TPU v7x, 32 devices: a whole 2x2x4 slice. The times are simulated.
32 devices in a mesh: row: 2 (over x), col: 4 (over y, core), dp: 4 (over z).
Axes of the slice: x: 2, y: 2, z: 4, core: 2. Of those that a mesh axis runs over, the one named last changes fastest.
Arguments:
- tokens: bfloat16 [8192, 1152], P('dp', 'col'), may hold values from -6 to 6
- positions: int32 [8192], P('dp'), may hold values from 0 to 1023, as said below
- prefix: int32 [8], replicated, may hold values from 102 to 512
- norm1_gain: bfloat16 [1152], P(('col', 'dp')), may hold values from 0.5 to 1.5
- query_key_value_weight: bfloat16 [1152, 1920], P(('col', 'dp'), 'row'), may hold values from -0.1875 to 0.1875
- out_weight: bfloat16 [1152, 1152], P('row', ('col', 'dp')), may hold values from -2 to 2
- norm2_gain: bfloat16 [1152], P(('col', 'dp')), may hold values from 0.5 to 1.5
- gate_up_weight: bfloat16 [1152, 6144], P(('col', 'dp'), 'row'), may hold values from -0.1875 to 0.1875
- down_weight: bfloat16 [3072, 1152], P('row', ('col', 'dp')), may hold values from -0.109375 to 0.109375
- cotangent: bfloat16 [8192, 1152], P('dp', 'col'), may hold values from -6 to 6
Outputs:
- output: bfloat16 [8192, 1152], P('dp', 'col')
- input_grad: float32 [8192, 1152], P('dp', 'col')
- norm1_grad: float32 [1152], P(('col', 'dp'))
- qkv_grad: float32 [1152, 1920], P(('col', 'dp'), 'row')
- out_grad: float32 [1152, 1152], P('row', ('col', 'dp'))
- norm2_grad: float32 [1152], P(('col', 'dp'))
- gate_up_grad: float32 [1152, 6144], P(('col', 'dp'), 'row')
- down_grad: float32 [3072, 1152], P('row', ('col', 'dp'))
Inputs may be any that keep to these rules, and one draw needn't show every extreme that they name: `positions`: within each sequence every place 0 to 1023 occurs once; the 256 rows of one sequence on one index of dp hold 256 consecutive places in increasing order, starting at a multiple of 256.
All inputs are finite; a program needn't handle non-finite values.
Results may differ from a plain program's by a relative error of at most 0.034.
Values may be sent and summed in bfloat16 or wider, within the bound.
A program may use at most 192 MiB of HBM per device.

v0:
```python
import jax
import jax.numpy as jnp
from jax import lax
from jax.sharding import PartitionSpec as P

MODEL_WIDTH = 1152
HEAD_SIZE = 64
SEG = 256
SEQ_MB = 2
MB = 4


EPSILON = 1e-05
THETA = 10000.0
MASKED = -1e30


def rope_tables(places):
    halfway = HEAD_SIZE // 2
    inverse = THETA ** (-(jnp.arange(halfway, dtype=jnp.float32) * 2.0 / HEAD_SIZE))
    angles = places.astype(jnp.float32)[:, None] * inverse[None, :]
    cosine = jnp.cos(angles)
    sine = jnp.sin(angles)
    return (jnp.concatenate([cosine, cosine], axis=-1), jnp.concatenate([sine, sine], axis=-1))


def turned(values):
    halfway = values.shape[-1] // 2
    return jnp.concatenate([-values[..., halfway:], values[..., :halfway]], axis=-1)


def rotate(values, cosine, sine):
    return values * cosine[:, None, :] + turned(values) * sine[:, None, :]


def unrotate(values, cosine, sine):
    return values * cosine[:, None, :] - turned(values * sine[:, None, :])


def row_total(values):
    return lax.psum(values, "col")


def row_sum(values):
    return lax.psum(values.astype(jnp.bfloat16), "row").astype(jnp.float32)


def col_rows(values):
    return lax.all_gather(values, "col", axis=0, tiled=True)


def col_sums(left, weight, contract):
    return lax.psum_scatter(
        lax.dot_general(
            left, weight, (((1,), (contract,)), ((), ())), preferred_element_type=jnp.float32
        ).astype(jnp.bfloat16),
        "col",
        scatter_dimension=0,
        tiled=True,
    ).astype(jnp.float32)


def gather_weights(gain_one, qkv_part, out_part, gain_two, gate_up_part, down_part):
    return (
        lax.all_gather(gain_one, "dp", axis=0, tiled=True),
        lax.all_gather(qkv_part, "dp", axis=0, tiled=True),
        lax.all_gather(out_part, "dp", axis=1, tiled=True),
        lax.all_gather(gain_two, "dp", axis=0, tiled=True),
        lax.all_gather(gate_up_part, "dp", axis=0, tiled=True),
        lax.all_gather(down_part, "dp", axis=1, tiled=True),
    )


def sum_grads(terms):
    grad_one, grad_qkv, grad_out, grad_two, grad_gate_up, grad_down = terms
    return (
        lax.psum_scatter(
            grad_one.astype(jnp.bfloat16), "dp", scatter_dimension=0, tiled=True
        ).astype(jnp.float32),
        lax.psum_scatter(
            grad_qkv.astype(jnp.bfloat16), "dp", scatter_dimension=0, tiled=True
        ).astype(jnp.float32),
        lax.psum_scatter(
            grad_out.astype(jnp.bfloat16), "dp", scatter_dimension=1, tiled=True
        ).astype(jnp.float32),
        lax.psum_scatter(
            grad_two.astype(jnp.bfloat16), "dp", scatter_dimension=0, tiled=True
        ).astype(jnp.float32),
        lax.psum_scatter(
            grad_gate_up.astype(jnp.bfloat16), "dp", scatter_dimension=0, tiled=True
        ).astype(jnp.float32),
        lax.psum_scatter(
            grad_down.astype(jnp.bfloat16), "dp", scatter_dimension=1, tiled=True
        ).astype(jnp.float32),
    )


def norm_forward(values, totaling):
    totals = totaling(jnp.sum(values * values, axis=1))
    scale = lax.rsqrt(totals / MODEL_WIDTH + EPSILON)
    return (values * scale[:, None], scale)


def norm_backward(normed, scale, gain, grad_normed, totaling):
    weighted = grad_normed * gain
    inner = totaling(jnp.sum(weighted * normed, axis=1)) / MODEL_WIDTH
    grad_in = scale[:, None] * (weighted - normed * inner[:, None])
    return (grad_in, jnp.sum(grad_normed * normed, axis=0))


def to_query_order(values, col_count, sub_rows):
    width = values.shape[1]
    shaped = values.reshape(SEQ_MB, col_count, sub_rows, width).transpose(1, 0, 2, 3)
    return shaped.reshape(SEQ_MB * col_count * sub_rows, width)


def from_query_order(values, col_count, sub_rows):
    width = values.shape[1]
    shaped = values.reshape(col_count, SEQ_MB, sub_rows, width).transpose(1, 0, 2, 3)
    return shaped.reshape(SEQ_MB * col_count * sub_rows, width)


def block_scores(queries, keys_values):
    key_value_heads = queries.shape[0]
    keys = keys_values[:, : key_value_heads * HEAD_SIZE].reshape(
        keys_values.shape[0], key_value_heads, HEAD_SIZE
    )
    return jnp.einsum(
        "hgqd,khd->hgqk", queries, keys, preferred_element_type=jnp.float32
    ) * HEAD_SIZE ** (-0.5)


def visible_mask(query_places, limit, key_places):
    return (key_places[None, :] <= query_places[:, None]) | (key_places[None, :] < limit)


def softmax_totals(queries, blocks, query_places, limit):
    shape = queries.shape[:3]

    def visit(carry, item):
        keys_values, key_places = item
        mask = visible_mask(query_places, limit, key_places)

        def compute(state):
            highest, summed = state
            scores = jnp.where(mask, block_scores(queries, keys_values), MASKED)
            fresh = jnp.maximum(highest, jnp.max(scores, axis=-1))
            summed = summed * jnp.exp(highest - fresh) + jnp.sum(
                jnp.exp(scores - fresh[..., None]), axis=-1
            )
            return (fresh, summed)

        def unchanged(state):
            return state

        return (lax.cond(jnp.any(mask), compute, unchanged, carry), None)

    start = (jnp.full(shape, MASKED, jnp.float32), jnp.zeros(shape, jnp.float32))
    (highest, summed), ignored = lax.scan(visit, start, blocks)
    return highest + jnp.log(summed)


def attend(queries, blocks, query_places, limit, log_totals):
    key_value_heads = queries.shape[0]

    def visit(carry, item):
        keys_values, key_places = item
        mask = visible_mask(query_places, limit, key_places)

        def compute(running):
            scores = jnp.where(mask, block_scores(queries, keys_values), MASKED)
            weights = jnp.exp(scores - log_totals[..., None]).astype(jnp.bfloat16)
            values = keys_values[:, key_value_heads * HEAD_SIZE :].reshape(
                keys_values.shape[0], key_value_heads, HEAD_SIZE
            )
            return running + jnp.einsum(
                "hgqk,khd->hgqd", weights, values, preferred_element_type=jnp.float32
            )

        def unchanged(running):
            return running

        return (lax.cond(jnp.any(mask), compute, unchanged, carry), None)

    result, ignored = lax.scan(visit, jnp.zeros(queries.shape, jnp.float32), blocks)
    return result


def attend_back(queries, blocks, query_places, limit, log_totals, grad_heads, delta):
    key_value_heads = queries.shape[0]

    def visit(carry, item):
        keys_values, key_places = item
        mask = visible_mask(query_places, limit, key_places)
        block_rows = keys_values.shape[0]

        def compute(grad_q):
            keys = keys_values[:, : key_value_heads * HEAD_SIZE].reshape(
                block_rows, key_value_heads, HEAD_SIZE
            )
            values = keys_values[:, key_value_heads * HEAD_SIZE :].reshape(
                block_rows, key_value_heads, HEAD_SIZE
            )
            scores = jnp.where(mask, block_scores(queries, keys_values), MASKED)
            probs = jnp.exp(scores - log_totals[..., None])
            grad_probs = jnp.einsum(
                "hgqd,khd->hgqk", grad_heads, values, preferred_element_type=jnp.float32
            )
            grad_scores = (probs * (grad_probs - delta[..., None])).astype(jnp.bfloat16)
            grad_q = grad_q + jnp.einsum(
                "hgqk,khd->hgqd", grad_scores, keys, preferred_element_type=jnp.float32
            )
            grad_keys = jnp.einsum(
                "hgqk,hgqd->khd", grad_scores, queries, preferred_element_type=jnp.float32
            ) * HEAD_SIZE ** (-0.5)
            grad_values = jnp.einsum(
                "hgqk,hgqd->khd",
                probs.astype(jnp.bfloat16),
                grad_heads,
                preferred_element_type=jnp.float32,
            )
            pieces = jnp.concatenate(
                [
                    grad_keys.reshape(block_rows, key_value_heads * HEAD_SIZE),
                    grad_values.reshape(block_rows, key_value_heads * HEAD_SIZE),
                ],
                axis=1,
            )
            return (grad_q, pieces)

        def skipped(grad_q):
            return (grad_q, jnp.zeros((block_rows, keys_values.shape[1]), jnp.float32))

        return lax.cond(jnp.any(mask), compute, skipped, carry)

    grad_q, pieces = lax.scan(visit, jnp.zeros(queries.shape, jnp.float32), blocks)
    return (
        grad_q * HEAD_SIZE ** (-0.5),
        pieces.reshape(pieces.shape[0] * pieces.shape[1], pieces.shape[2]),
    )


def shards(
    tokens,
    positions,
    prefix,
    norm1_gain,
    query_key_value_weight,
    out_weight,
    norm2_gain,
    gate_up_weight,
    down_weight,
    cotangent,
):
    col_count = lax.axis_size("col")
    data_count = lax.axis_size("dp")
    col_place = lax.axis_index("col")
    batch_rows = SEQ_MB * SEG
    sub_rows = SEG // col_count
    query_rows = SEQ_MB * sub_rows
    query_head_count = out_weight.shape[0] // HEAD_SIZE
    key_value_heads = (query_key_value_weight.shape[1] - query_head_count * HEAD_SIZE) // (
        2 * HEAD_SIZE
    )
    query_group = query_head_count // key_value_heads
    hidden = down_weight.shape[0]
    senders = col_count * data_count
    key_count = senders * sub_rows
    key_block = 512
    block_count = key_count // key_block
    all_places = lax.all_gather(positions, "dp", axis=0, tiled=True)
    place_table = all_places.reshape(data_count, MB, SEQ_MB, col_count, sub_rows)
    local_table = positions.reshape(MB, SEQ_MB, col_count, sub_rows)
    start = (
        jnp.zeros((norm1_gain.shape[0] * data_count,), jnp.float32),
        jnp.zeros(
            (query_key_value_weight.shape[0] * data_count, query_key_value_weight.shape[1]),
            jnp.float32,
        ),
        jnp.zeros((out_weight.shape[0], out_weight.shape[1] * data_count), jnp.float32),
        jnp.zeros((norm2_gain.shape[0] * data_count,), jnp.float32),
        jnp.zeros((gate_up_weight.shape[0] * data_count, gate_up_weight.shape[1]), jnp.float32),
        jnp.zeros((down_weight.shape[0], down_weight.shape[1] * data_count), jnp.float32),
    )

    def micro_batch(carry, item):
        batch, batch_tokens, batch_cotangent = item
        ordered_tokens = to_query_order(batch_tokens, col_count, sub_rows)
        ordered_cotangent = to_query_order(batch_cotangent, col_count, sub_rows)
        gathered = gather_weights(
            norm1_gain, query_key_value_weight, out_weight, norm2_gain, gate_up_weight, down_weight
        )
        rows_tokens, rows_cotangent = (ordered_tokens, ordered_cotangent)
        gain_one, qkv_full, out_full, gain_two, gate_up_full, down_full = gathered
        gain_one = gain_one.astype(jnp.float32)
        gain_two = gain_two.astype(jnp.float32)
        rows_in = rows_tokens.astype(jnp.float32)
        normed_one, scale_one = norm_forward(rows_in, row_total)
        input_one = (normed_one * gain_one).astype(jnp.bfloat16)
        mixed = col_sums(input_one, qkv_full, 0)
        batch_local = lax.dynamic_index_in_dim(local_table, batch, 0, keepdims=False)
        query_places = lax.dynamic_index_in_dim(batch_local, col_place, 1, keepdims=False)
        batch_places = lax.dynamic_index_in_dim(place_table, batch, 1, keepdims=False)
        cosine, sine = rope_tables(query_places.reshape(query_rows))
        query_raw = mixed[:, : query_head_count * HEAD_SIZE].reshape(
            query_rows, query_head_count, HEAD_SIZE
        )
        key_unrotated = mixed[
            :, query_head_count * HEAD_SIZE : (query_head_count + key_value_heads) * HEAD_SIZE
        ].reshape(query_rows, key_value_heads, HEAD_SIZE)
        value_unshaped = mixed[:, (query_head_count + key_value_heads) * HEAD_SIZE :]
        queries = rotate(query_raw, cosine, sine).astype(jnp.bfloat16)
        keys = rotate(key_unrotated, cosine, sine).astype(jnp.bfloat16)
        keys_values = jnp.concatenate(
            [
                keys.reshape(query_rows, key_value_heads * HEAD_SIZE),
                value_unshaped.astype(jnp.bfloat16),
            ],
            axis=1,
        )
        kv_width = keys_values.shape[1]
        everyone = lax.all_gather(keys_values, ("col", "dp"), axis=0, tiled=True)
        query_heads = queries.reshape(
            query_rows, key_value_heads, query_group, HEAD_SIZE
        ).transpose(1, 2, 0, 3)
        limits = []
        place_blocks = []
        for member in range(SEQ_MB):
            limits.append(
                lax.dynamic_index_in_dim(prefix, batch * SEQ_MB + member, 0, keepdims=False)
            )
            member_places = batch_places[:, member].transpose(1, 0, 2).reshape(key_count)
            place_blocks.append(member_places.reshape(block_count, key_block))

        def member_keys(table, member):
            chosen = table.reshape(senders, SEQ_MB, sub_rows, kv_width)[:, member]
            return chosen.reshape(block_count, key_block, kv_width)

        log_parts = []
        head_parts = []
        for member in range(SEQ_MB):
            lower = member * sub_rows
            member_queries = query_heads[:, :, lower : lower + sub_rows]
            blocks = (member_keys(everyone, member), place_blocks[member])
            member_logs = softmax_totals(
                member_queries, blocks, query_places[member], limits[member]
            )
            log_parts.append(member_logs)
            head_parts.append(
                attend(member_queries, blocks, query_places[member], limits[member], member_logs)
            )
        log_totals = jnp.concatenate(log_parts, axis=2)
        heads_out = jnp.concatenate(head_parts, axis=2).astype(jnp.bfloat16)
        heads_flat = heads_out.transpose(2, 0, 1, 3).reshape(
            query_rows, query_head_count * HEAD_SIZE
        )
        heads_rows = col_rows(heads_flat)
        middle = rows_in + row_sum(
            jnp.dot(heads_rows, out_full, preferred_element_type=jnp.float32)
        )
        normed_two, scale_two = norm_forward(middle, row_total)
        input_two = (normed_two * gain_two).astype(jnp.bfloat16)
        gate_up = col_sums(input_two, gate_up_full, 0)
        gate = gate_up[:, :hidden]
        upward = gate_up[:, hidden:]
        sigma = jax.nn.sigmoid(gate)
        active = (gate * sigma * upward).astype(jnp.bfloat16)
        active_rows = col_rows(active)
        result = middle + row_sum(
            jnp.dot(active_rows, down_full, preferred_element_type=jnp.float32)
        )
        grad_down = lax.dot_general(
            active_rows,
            rows_cotangent,
            (((0,), (0,)), ((), ())),
            preferred_element_type=jnp.float32,
        )
        grad_active = col_sums(rows_cotangent, down_full, 1)
        grad_gate = grad_active * upward * sigma * (1.0 + gate * (1.0 - sigma))
        grad_up = grad_active * gate * sigma
        grad_mix = jnp.concatenate([grad_gate, grad_up], axis=1).astype(jnp.bfloat16)
        grad_mix_rows = col_rows(grad_mix)
        grad_gate_up = lax.dot_general(
            input_two, grad_mix_rows, (((0,), (0,)), ((), ())), preferred_element_type=jnp.float32
        )
        grad_normed_two = row_sum(
            lax.dot_general(
                grad_mix_rows,
                gate_up_full,
                (((1,), (1,)), ((), ())),
                preferred_element_type=jnp.float32,
            )
        )
        back_two, grad_gain_two = norm_backward(
            normed_two, scale_two, gain_two, grad_normed_two, row_total
        )
        grad_middle = rows_cotangent.astype(jnp.float32) + back_two
        grad_branch = grad_middle.astype(jnp.bfloat16)
        grad_out = lax.dot_general(
            heads_rows, grad_branch, (((0,), (0,)), ((), ())), preferred_element_type=jnp.float32
        )
        grad_flat = col_sums(grad_branch, out_full, 1).astype(jnp.bfloat16)
        grad_heads = grad_flat.reshape(
            query_rows, key_value_heads, query_group, HEAD_SIZE
        ).transpose(1, 2, 0, 3)
        delta = jnp.sum(grad_heads.astype(jnp.float32) * heads_out.astype(jnp.float32), axis=-1)
        again = lax.all_gather(keys_values, ("col", "dp"), axis=0, tiled=True)
        grad_q_parts = []
        piece_parts = []
        for member in range(SEQ_MB):
            lower = member * sub_rows
            blocks = (member_keys(again, member), place_blocks[member])
            member_grad_q, member_pieces = attend_back(
                query_heads[:, :, lower : lower + sub_rows],
                blocks,
                query_places[member],
                limits[member],
                log_totals[:, :, lower : lower + sub_rows],
                grad_heads[:, :, lower : lower + sub_rows],
                delta[:, :, lower : lower + sub_rows],
            )
            grad_q_parts.append(member_grad_q)
            piece_parts.append(member_pieces.reshape(senders, sub_rows, kv_width))
        grad_q = jnp.concatenate(grad_q_parts, axis=2)
        grad_kv_all = jnp.stack(piece_parts, axis=1).reshape(senders * query_rows, kv_width)
        grad_kv = lax.psum_scatter(grad_kv_all, ("col", "dp"), scatter_dimension=0, tiled=True)
        grad_keys = unrotate(
            grad_kv[:, : key_value_heads * HEAD_SIZE].reshape(
                query_rows, key_value_heads, HEAD_SIZE
            ),
            cosine,
            sine,
        )
        grad_queries = unrotate(
            grad_q.transpose(2, 0, 1, 3).reshape(query_rows, query_head_count, HEAD_SIZE),
            cosine,
            sine,
        )
        grad_mixed = jnp.concatenate(
            [
                grad_queries.reshape(query_rows, query_head_count * HEAD_SIZE),
                grad_keys.reshape(query_rows, key_value_heads * HEAD_SIZE),
                grad_kv[:, key_value_heads * HEAD_SIZE :],
            ],
            axis=1,
        ).astype(jnp.bfloat16)
        grad_mixed_rows = col_rows(grad_mixed)
        grad_qkv = lax.dot_general(
            input_one, grad_mixed_rows, (((0,), (0,)), ((), ())), preferred_element_type=jnp.float32
        )
        grad_normed_one = row_sum(
            lax.dot_general(
                grad_mixed_rows,
                qkv_full,
                (((1,), (1,)), ((), ())),
                preferred_element_type=jnp.float32,
            )
        )
        back_one, grad_gain_one = norm_backward(
            normed_one, scale_one, gain_one, grad_normed_one, row_total
        )
        grad_input = grad_middle + back_one
        result_low = result.astype(jnp.bfloat16)
        terms = (grad_gain_one, grad_qkv, grad_out, grad_gain_two, grad_gate_up, grad_down)
        carry = jax.tree.map(jnp.add, carry, terms)
        return (
            carry,
            (
                from_query_order(result_low, col_count, sub_rows),
                from_query_order(grad_input, col_count, sub_rows),
            ),
        )

    batch_items = (
        jnp.arange(MB, dtype=jnp.int32),
        tokens.reshape(MB, batch_rows, tokens.shape[1]),
        cotangent.reshape(MB, batch_rows, cotangent.shape[1]),
    )
    totals, (results, input_grads) = lax.scan(micro_batch, start, batch_items)
    totals = sum_grads(totals)
    output = results.reshape(tokens.shape)
    input_grad = input_grads.reshape(tokens.shape)
    return (output, input_grad, totals[0], totals[1], totals[2], totals[3], totals[4], totals[5])


def solution(mesh):
    in_specs = (
        P("dp", "col"),
        P("dp"),
        P(),
        P(("col", "dp")),
        P(("col", "dp"), "row"),
        P("row", ("col", "dp")),
        P(("col", "dp")),
        P(("col", "dp"), "row"),
        P("row", ("col", "dp")),
        P("dp", "col"),
    )
    out_specs = (
        P("dp", "col"),
        P("dp", "col"),
        P(("col", "dp")),
        P(("col", "dp"), "row"),
        P("row", ("col", "dp")),
        P(("col", "dp")),
        P(("col", "dp"), "row"),
        P("row", ("col", "dp")),
    )
    return jax.shard_map(shards, mesh=mesh, in_specs=in_specs, out_specs=out_specs, check_vma=False)
```

profile of v0, /device:TPU:13, one launch (start us, length us, event | category | flops | bytes accessed | tf_op | source)
XLA Modules:
  0.0 2239.6 jit_solution(1807750820518253790)
XLA Ops:
  23.9 2095.7 %while.208 = (s32[]{:T(128)}, f32[288]{0:T(512)}, f32[288,960]{1,0:T(8,128)}, f32[576,288]{0,1:T(8,128)}, f32[288]{0:T(512)}, /*index=5*/f32[288,3072]{1,0:T(8,1...) while((s32[]{:T(128)}, f32[288]{0:T(512)}, ...), condition=%wide.region_55.56_spmd.clone, body=%wide.region_0.55_spmd.clone.sunk | while | flops 6076643840 | bytes 305429152 | solution.py:479
  108.0 24.9 %all-gather.5.cloned.1.call-done = bf16[2048,384]{0,1:T(8,128)(2,1)} async-done(((bf16[128,384]{0,1:T(8,128)(2,1)}), bf16[2048,384]{0,1:T(8,128)(2,1)}) %all-gather.5.cloned.1.call-update) | async-done | bytes 1572880 | tf_op jit(solution)/shard_map/while/body/eval_jaxpr/all_gather | solution.py:407
  179.7 21.9 all-reduce.18.cloned.1.call-done
  263.6 28.0 %reduce-scatter.30.cloned.1.call-done = bf16[128,1536]{1,0:T(8,128)(2,1)} async-done(((bf16[512,1536]{1,0:T(8,128)(2,1)}), bf16[128,1536]{1,0:T(8,128)(2,1)}) %reduce-scatter.30.cloned.1.call-update) | async-done | bytes 393232 | tf_op jit(solution)/shard_map/while/body/eval_jaxpr/reduce_scatter | solution.py:53
  295.3 29.2 %all-gather.9.cloned.1.call-done = bf16[512,3072]{1,0:T(8,128)(2,1)} async-done(((bf16[128,3072]{1,0:T(8,128)(2,1)}), bf16[512,3072]{1,0:T(8,128)(2,1)}) %all-gather.9.cloned.1.call-update) | async-done | bytes 3145744 | tf_op jit(solution)/shard_map/while/body/eval_jaxpr/all_gather | solution.py:49
  329.0 23.7 %all-reduce.20.cloned.1.call-done = bf16[512,288]{0,1:T(8,128)(2,1)} async-done(((bf16[512,288]{0,1:T(8,128)(2,1)}), bf16[512,288]{0,1:T(8,128)(2,1)}) %all-reduce.20.cloned.1.call-update) | async-done | bytes 294928 | tf_op jit(solution)/shard_map/while/body/eval_jaxpr/psum | solution.py:45
  439.1 53.7 %reduce-scatter.36.cloned.1.call-done = f32[128,384]{0,1:T(8,128)} async-done(((f32[2048,384]{0,1:T(8,128)}), f32[128,384]{0,1:T(8,128)}) %reduce-scatter.36.cloned.1.call-update) | async-done | bytes 196624 | tf_op jit(solution)/shard_map/while/body/eval_jaxpr/reduce_scatter | solution.py:426
  511.0 26.7 %all-reduce.22.cloned.1.call-done = (bf16[512,288]{0,1:T(8,128)(2,1)}, bf16[512,288]{0,1:T(8,128)(2,1)}) async-done(((bf16[512,288]{0,1:T(8,128)(2,1)}, bf16[512,288]{0,1:T(8,128)(2,1)}), (bf16[512,288]{0,1:T(8,128)(2,1)}, bf16[512,288]{0,1:T(8,128)(2,1)})) %all-reduce.22.cloned.1.call-update) | async-done | bytes 589840 | tf_op jit(solution)/shard_map/while/body/eval_jaxpr/psum | solution.py:45
  631.3 25.0 %all-gather.5.cloned.1.call-done = bf16[2048,384]{0,1:T(8,128)(2,1)} async-done(((bf16[128,384]{0,1:T(8,128)(2,1)}), bf16[2048,384]{0,1:T(8,128)(2,1)}) %all-gather.5.cloned.1.call-update) | async-done | bytes 1572880 | tf_op jit(solution)/shard_map/while/body/eval_jaxpr/all_gather | solution.py:407
  703.0 21.9 all-reduce.18.cloned.1.call-done
  786.9 28.0 %reduce-scatter.30.cloned.1.call-done = bf16[128,1536]{1,0:T(8,128)(2,1)} async-done(((bf16[512,1536]{1,0:T(8,128)(2,1)}), bf16[128,1536]{1,0:T(8,128)(2,1)}) %reduce-scatter.30.cloned.1.call-update) | async-done | bytes 393232 | tf_op jit(solution)/shard_map/while/body/eval_jaxpr/reduce_scatter | solution.py:53
  818.6 29.2 %all-gather.9.cloned.1.call-done = bf16[512,3072]{1,0:T(8,128)(2,1)} async-done(((bf16[128,3072]{1,0:T(8,128)(2,1)}), bf16[512,3072]{1,0:T(8,128)(2,1)}) %all-gather.9.cloned.1.call-update) | async-done | bytes 3145744 | tf_op jit(solution)/shard_map/while/body/eval_jaxpr/all_gather | solution.py:49
  852.3 23.7 %all-reduce.20.cloned.1.call-done = bf16[512,288]{0,1:T(8,128)(2,1)} async-done(((bf16[512,288]{0,1:T(8,128)(2,1)}), bf16[512,288]{0,1:T(8,128)(2,1)}) %all-reduce.20.cloned.1.call-update) | async-done | bytes 294928 | tf_op jit(solution)/shard_map/while/body/eval_jaxpr/psum | solution.py:45
  964.5 51.7 %reduce-scatter.36.cloned.1.call-done = f32[128,384]{0,1:T(8,128)} async-done(((f32[2048,384]{0,1:T(8,128)}), f32[128,384]{0,1:T(8,128)}) %reduce-scatter.36.cloned.1.call-update) | async-done | bytes 196624 | tf_op jit(solution)/shard_map/while/body/eval_jaxpr/reduce_scatter | solution.py:426
  1036.9 24.2 %all-reduce.22.cloned.1.call-done = (bf16[512,288]{0,1:T(8,128)(2,1)}, bf16[512,288]{0,1:T(8,128)(2,1)}) async-done(((bf16[512,288]{0,1:T(8,128)(2,1)}, bf16[512,288]{0,1:T(8,128)(2,1)}), (bf16[512,288]{0,1:T(8,128)(2,1)}, bf16[512,288]{0,1:T(8,128)(2,1)})) %all-reduce.22.cloned.1.call-update) | async-done | bytes 589840 | tf_op jit(solution)/shard_map/while/body/eval_jaxpr/psum | solution.py:45
  1113.8 21.8 reduce-scatter.28.cloned.1.call-done
  1154.6 25.2 %all-gather.5.cloned.1.call-done = bf16[2048,384]{0,1:T(8,128)(2,1)} async-done(((bf16[128,384]{0,1:T(8,128)(2,1)}), bf16[2048,384]{0,1:T(8,128)(2,1)}) %all-gather.5.cloned.1.call-update) | async-done | bytes 1572880 | tf_op jit(solution)/shard_map/while/body/eval_jaxpr/all_gather | solution.py:407
  1226.5 21.9 all-reduce.18.cloned.1.call-done
  1310.4 28.0 %reduce-scatter.30.cloned.1.call-done = bf16[128,1536]{1,0:T(8,128)(2,1)} async-done(((bf16[512,1536]{1,0:T(8,128)(2,1)}), bf16[128,1536]{1,0:T(8,128)(2,1)}) %reduce-scatter.30.cloned.1.call-update) | async-done | bytes 393232 | tf_op jit(solution)/shard_map/while/body/eval_jaxpr/reduce_scatter | solution.py:53
  1342.1 29.2 %all-gather.9.cloned.1.call-done = bf16[512,3072]{1,0:T(8,128)(2,1)} async-done(((bf16[128,3072]{1,0:T(8,128)(2,1)}), bf16[512,3072]{1,0:T(8,128)(2,1)}) %all-gather.9.cloned.1.call-update) | async-done | bytes 3145744 | tf_op jit(solution)/shard_map/while/body/eval_jaxpr/all_gather | solution.py:49
  1375.8 23.7 %all-reduce.20.cloned.1.call-done = bf16[512,288]{0,1:T(8,128)(2,1)} async-done(((bf16[512,288]{0,1:T(8,128)(2,1)}), bf16[512,288]{0,1:T(8,128)(2,1)}) %all-reduce.20.cloned.1.call-update) | async-done | bytes 294928 | tf_op jit(solution)/shard_map/while/body/eval_jaxpr/psum | solution.py:45
  1487.9 51.6 %reduce-scatter.36.cloned.1.call-done = f32[128,384]{0,1:T(8,128)} async-done(((f32[2048,384]{0,1:T(8,128)}), f32[128,384]{0,1:T(8,128)}) %reduce-scatter.36.cloned.1.call-update) | async-done | bytes 196624 | tf_op jit(solution)/shard_map/while/body/eval_jaxpr/reduce_scatter | solution.py:426
  1560.3 24.2 %all-reduce.22.cloned.1.call-done = (bf16[512,288]{0,1:T(8,128)(2,1)}, bf16[512,288]{0,1:T(8,128)(2,1)}) async-done(((bf16[512,288]{0,1:T(8,128)(2,1)}, bf16[512,288]{0,1:T(8,128)(2,1)}), (bf16[512,288]{0,1:T(8,128)(2,1)}, bf16[512,288]{0,1:T(8,128)(2,1)})) %all-reduce.22.cloned.1.call-update) | async-done | bytes 589840 | tf_op jit(solution)/shard_map/while/body/eval_jaxpr/psum | solution.py:45
  1678.1 24.9 %all-gather.5.cloned.1.call-done = bf16[2048,384]{0,1:T(8,128)(2,1)} async-done(((bf16[128,384]{0,1:T(8,128)(2,1)}), bf16[2048,384]{0,1:T(8,128)(2,1)}) %all-gather.5.cloned.1.call-update) | async-done | bytes 1572880 | tf_op jit(solution)/shard_map/while/body/eval_jaxpr/all_gather | solution.py:407
  1749.9 21.8 all-reduce.18.cloned.1.call-done
  1834.0 28.2 %reduce-scatter.30.cloned.1.call-done = bf16[128,1536]{1,0:T(8,128)(2,1)} async-done(((bf16[512,1536]{1,0:T(8,128)(2,1)}), bf16[128,1536]{1,0:T(8,128)(2,1)}) %reduce-scatter.30.cloned.1.call-update) | async-done | bytes 393232 | tf_op jit(solution)/shard_map/while/body/eval_jaxpr/reduce_scatter | solution.py:53
  1865.9 29.2 %all-gather.9.cloned.1.call-done = bf16[512,3072]{1,0:T(8,128)(2,1)} async-done(((bf16[128,3072]{1,0:T(8,128)(2,1)}), bf16[512,3072]{1,0:T(8,128)(2,1)}) %all-gather.9.cloned.1.call-update) | async-done | bytes 3145744 | tf_op jit(solution)/shard_map/while/body/eval_jaxpr/all_gather | solution.py:49
  1899.5 23.7 %all-reduce.20.cloned.1.call-done = bf16[512,288]{0,1:T(8,128)(2,1)} async-done(((bf16[512,288]{0,1:T(8,128)(2,1)}), bf16[512,288]{0,1:T(8,128)(2,1)}) %all-reduce.20.cloned.1.call-update) | async-done | bytes 294928 | tf_op jit(solution)/shard_map/while/body/eval_jaxpr/psum | solution.py:45
  2011.7 51.6 %reduce-scatter.36.cloned.1.call-done = f32[128,384]{0,1:T(8,128)} async-done(((f32[2048,384]{0,1:T(8,128)}), f32[128,384]{0,1:T(8,128)}) %reduce-scatter.36.cloned.1.call-update) | async-done | bytes 196624 | tf_op jit(solution)/shard_map/while/body/eval_jaxpr/reduce_scatter | solution.py:426
  2084.0 24.2 %all-reduce.22.cloned.1.call-done = (bf16[512,288]{0,1:T(8,128)(2,1)}, bf16[512,288]{0,1:T(8,128)(2,1)}) async-done(((bf16[512,288]{0,1:T(8,128)(2,1)}, bf16[512,288]{0,1:T(8,128)(2,1)}), (bf16[512,288]{0,1:T(8,128)(2,1)}, bf16[512,288]{0,1:T(8,128)(2,1)})) %all-reduce.22.cloned.1.call-update) | async-done | bytes 589840 | tf_op jit(solution)/shard_map/while/body/eval_jaxpr/psum | solution.py:45
  2165.0 25.3 %reduce-scatter.24.cloned.1.call-done = bf16[1536,72]{0,1:T(8,128)(2,1)} async-done(((bf16[1536,288]{0,1:T(8,128)(2,1)}), bf16[1536,72]{0,1:T(8,128)(2,1)}) %reduce-scatter.24.cloned.1.call-update) | async-done | bytes 221200 | tf_op jit(solution)/shard_map/reduce_scatter | solution.py:92
  2192.1 38.4 %reduce-scatter.22.cloned.1.call-done = bf16[72,3072]{1,0:T(8,128)(2,1)} async-done(((bf16[288,3072]{1,0:T(8,128)(2,1)}), bf16[72,3072]{1,0:T(8,128)(2,1)}) %reduce-scatter.22.cloned.1.call-update) | async-done | bytes 442384 | tf_op jit(solution)/shard_map/reduce_scatter | solution.py:89
  (1714 shorter events, 1619.2 us)
Async XLA Ops:
  23.9 64.9 %reduce-scatter.28.cloned.1.call-start = ((), (), s32[]{:S(2)}) async-start(), calls=%async_computation.13 | async-start | bytes 1310720 | tf_op jit(solution)/shard_map/while
  64.9 68.0 %all-gather.5.cloned.1.call-start = ((), (), s32[]{:S(2)}) async-start(), calls=%async_computation.14 | async-start | bytes 1671168 | tf_op jit(solution)/shard_map/while/body/eval_jaxpr/all_gather | solution.py:407
  90.8 110.9 %all-reduce.18.cloned.1.call-start = ((), (), s32[]{:S(2)}) async-start(), calls=%async_computation.17 | async-start | bytes 589824 | tf_op jit(solution)/shard_map/while/body/eval_jaxpr/psum | solution.py:45
  179.6 81.5 %reduce-scatter.32.cloned.1.call-start = ((), (), s32[]{:S(2)}) async-start(), calls=%async_computation.18 | async-start | bytes 3932160 | tf_op jit(solution)/shard_map/while/body/eval_jaxpr/reduce_scatter | solution.py:53
  223.7 67.9 %reduce-scatter.30.cloned.1.call-start = ((), (), s32[]{:S(2)}) async-start(), calls=%async_computation.15 | async-start | bytes 1966080 | tf_op jit(solution)/shard_map/while/body/eval_jaxpr/reduce_scatter | solution.py:53
  245.5 79.0 %all-gather.9.cloned.1.call-start = ((), (), s32[]{:S(2)}) async-start(), calls=%async_computation.19 | async-start | bytes 3932160 | tf_op jit(solution)/shard_map/while/body/eval_jaxpr/all_gather | solution.py:49
  363.5 64.1 %all-gather.11.cloned.1.call-start = ((), (), s32[]{:S(2)}) async-start(), calls=%async_computation.23 | async-start | bytes 1966080 | tf_op jit(solution)/shard_map/while/body/eval_jaxpr/all_gather | solution.py:49
  364.3 128.5 %reduce-scatter.36.cloned.1.call-start = ((), (), s32[]{:S(2)}) async-start(), calls=%async_computation.22 | async-start | bytes 3342336 | tf_op jit(solution)/shard_map/while/body/eval_jaxpr/reduce_scatter | solution.py:426
  427.5 110.2 %all-reduce.22.cloned.1.call-start = ((), (), s32[]{:S(2)}) async-start(), calls=%async_computation.24 | async-start | bytes 1179648 | tf_op jit(solution)/shard_map/while/body/eval_jaxpr/psum | solution.py:45
  587.6 68.7 %all-gather.5.cloned.1.call-start = ((), (), s32[]{:S(2)}) async-start(), calls=%async_computation.14 | async-start | bytes 1671168 | tf_op jit(solution)/shard_map/while/body/eval_jaxpr/all_gather | solution.py:407
  614.1 110.9 %all-reduce.18.cloned.1.call-start = ((), (), s32[]{:S(2)}) async-start(), calls=%async_computation.17 | async-start | bytes 589824 | tf_op jit(solution)/shard_map/while/body/eval_jaxpr/psum | solution.py:45
  702.9 81.5 %reduce-scatter.32.cloned.1.call-start = ((), (), s32[]{:S(2)}) async-start(), calls=%async_computation.18 | async-start | bytes 3932160 | tf_op jit(solution)/shard_map/while/body/eval_jaxpr/reduce_scatter | solution.py:53
  747.0 67.9 %reduce-scatter.30.cloned.1.call-start = ((), (), s32[]{:S(2)}) async-start(), calls=%async_computation.15 | async-start | bytes 1966080 | tf_op jit(solution)/shard_map/while/body/eval_jaxpr/reduce_scatter | solution.py:53
  768.8 79.1 %all-gather.9.cloned.1.call-start = ((), (), s32[]{:S(2)}) async-start(), calls=%async_computation.19 | async-start | bytes 3932160 | tf_op jit(solution)/shard_map/while/body/eval_jaxpr/all_gather | solution.py:49
  887.5 128.7 %reduce-scatter.36.cloned.1.call-start = ((), (), s32[]{:S(2)}) async-start(), calls=%async_computation.22 | async-start | bytes 3342336 | tf_op jit(solution)/shard_map/while/body/eval_jaxpr/reduce_scatter | solution.py:426
  950.9 110.3 %all-reduce.22.cloned.1.call-start = ((), (), s32[]{:S(2)}) async-start(), calls=%async_computation.24 | async-start | bytes 1179648 | tf_op jit(solution)/shard_map/while/body/eval_jaxpr/psum | solution.py:45
  1110.9 68.9 %all-gather.5.cloned.1.call-start = ((), (), s32[]{:S(2)}) async-start(), calls=%async_computation.14 | async-start | bytes 1671168 | tf_op jit(solution)/shard_map/while/body/eval_jaxpr/all_gather | solution.py:407
  1137.5 110.9 %all-reduce.18.cloned.1.call-start = ((), (), s32[]{:S(2)}) async-start(), calls=%async_computation.17 | async-start | bytes 589824 | tf_op jit(solution)/shard_map/while/body/eval_jaxpr/psum | solution.py:45
  1226.4 81.5 %reduce-scatter.32.cloned.1.call-start = ((), (), s32[]{:S(2)}) async-start(), calls=%async_computation.18 | async-start | bytes 3932160 | tf_op jit(solution)/shard_map/while/body/eval_jaxpr/reduce_scatter | solution.py:53
  1270.5 67.9 %reduce-scatter.30.cloned.1.call-start = ((), (), s32[]{:S(2)}) async-start(), calls=%async_computation.15 | async-start | bytes 1966080 | tf_op jit(solution)/shard_map/while/body/eval_jaxpr/reduce_scatter | solution.py:53
  1292.2 79.0 %all-gather.9.cloned.1.call-start = ((), (), s32[]{:S(2)}) async-start(), calls=%async_computation.19 | async-start | bytes 3932160 | tf_op jit(solution)/shard_map/while/body/eval_jaxpr/all_gather | solution.py:49
  1411.0 128.5 %reduce-scatter.36.cloned.1.call-start = ((), (), s32[]{:S(2)}) async-start(), calls=%async_computation.22 | async-start | bytes 3342336 | tf_op jit(solution)/shard_map/while/body/eval_jaxpr/reduce_scatter | solution.py:426
  1474.3 110.2 %all-reduce.22.cloned.1.call-start = ((), (), s32[]{:S(2)}) async-start(), calls=%async_computation.24 | async-start | bytes 1179648 | tf_op jit(solution)/shard_map/while/body/eval_jaxpr/psum | solution.py:45
  1634.3 68.7 %all-gather.5.cloned.1.call-start = ((), (), s32[]{:S(2)}) async-start(), calls=%async_computation.14 | async-start | bytes 1671168 | tf_op jit(solution)/shard_map/while/body/eval_jaxpr/all_gather | solution.py:407
  1660.9 110.9 %all-reduce.18.cloned.1.call-start = ((), (), s32[]{:S(2)}) async-start(), calls=%async_computation.17 | async-start | bytes 589824 | tf_op jit(solution)/shard_map/while/body/eval_jaxpr/psum | solution.py:45
  1749.9 81.7 %reduce-scatter.32.cloned.1.call-start = ((), (), s32[]{:S(2)}) async-start(), calls=%async_computation.18 | async-start | bytes 3932160 | tf_op jit(solution)/shard_map/while/body/eval_jaxpr/reduce_scatter | solution.py:53
  1794.1 68.0 %reduce-scatter.30.cloned.1.call-start = ((), (), s32[]{:S(2)}) async-start(), calls=%async_computation.15 | async-start | bytes 1966080 | tf_op jit(solution)/shard_map/while/body/eval_jaxpr/reduce_scatter | solution.py:53
  1815.8 79.2 %all-gather.9.cloned.1.call-start = ((), (), s32[]{:S(2)}) async-start(), calls=%async_computation.19 | async-start | bytes 3932160 | tf_op jit(solution)/shard_map/while/body/eval_jaxpr/all_gather | solution.py:49
  1934.8 128.5 %reduce-scatter.36.cloned.1.call-start = ((), (), s32[]{:S(2)}) async-start(), calls=%async_computation.22 | async-start | bytes 3342336 | tf_op jit(solution)/shard_map/while/body/eval_jaxpr/reduce_scatter | solution.py:426
  1998.1 110.2 %all-reduce.22.cloned.1.call-start = ((), (), s32[]{:S(2)}) async-start(), calls=%async_computation.24 | async-start | bytes 1179648 | tf_op jit(solution)/shard_map/while/body/eval_jaxpr/psum | solution.py:45
  2124.0 66.4 %reduce-scatter.24.cloned.1.call-start = ((), (), s32[]{:S(2)}) async-start(), calls=%async_computation.11 | async-start | bytes 1105920 | tf_op jit(solution)/shard_map/reduce_scatter | solution.py:92
  2125.0 105.5 %reduce-scatter.22.cloned.1.call-start = ((), (), s32[]{:S(2)}) async-start(), calls=%async_computation.10 | async-start | bytes 2211840 | tf_op jit(solution)/shard_map/reduce_scatter | solution.py:89
  (296 other events, 6655.1 us)
Sparse Core Ops, SparseCore 0:
  65.0 23.7 reduce-scatter.27
  91.5 41.4 all-gather.4
  223.8 37.2 reduce-scatter.31
  263.5 28.0 reduce-scatter.29
  295.4 29.0 all-gather.8
  328.9 23.7 all-reduce.19
  427.7 65.0 reduce-scatter.35
  508.2 29.5 all-reduce.21
  587.7 24.4 reduce-scatter.27
  614.8 41.4 all-gather.4
  747.1 37.2 reduce-scatter.31
  786.8 28.0 reduce-scatter.29
  818.7 29.0 all-gather.8
  852.2 23.8 all-reduce.19
  951.0 65.1 reduce-scatter.35
  1031.6 29.5 all-reduce.21
  1111.0 24.4 reduce-scatter.27
  1138.0 41.6 all-gather.4
  1270.6 37.2 reduce-scatter.31
  1310.3 28.0 reduce-scatter.29
  1342.1 29.0 all-gather.8
  1375.7 23.7 all-reduce.19
  1474.4 65.0 reduce-scatter.35
  1555.0 29.4 all-reduce.21
  1634.5 24.4 reduce-scatter.27
  1661.6 41.4 all-gather.4
  1794.2 37.2 reduce-scatter.31
  1834.0 28.0 reduce-scatter.29
  1865.9 29.0 all-gather.8
  1899.4 23.7 all-reduce.19
  1998.2 65.0 reduce-scatter.35
  2078.7 29.4 all-reduce.21
  (12 shorter events, 256.1 us)
Sparse Core Ops, SparseCore 1:
  181.1 37.5 all-gather.6
  704.4 37.5 all-gather.6
  1227.8 37.5 all-gather.6
  1751.5 37.5 all-gather.6
  2123.3 16.0 reduce-scatter.25
  2141.6 21.7 reduce-scatter.19
  2166.1 24.2 reduce-scatter.23
  2192.6 37.9 reduce-scatter.21
where the time goes:
time: 2250 us; the launch traced here: 2240 us
  waiting for transfers between devices  1180 us (52%)
  blocking collectives  416 us (18%)
  matrix products  210 us (9%)
  other arithmetic  186 us (8%)
  local copies, waits for them, and re-layouts  177 us (8%)
  loops' own time  52.7 us (2%)
    psum x12, waiting for transfers between devices, row_sum(): return lax.psum(values.astype(jnp.bfloat16), 'row').astype(jnp.float32)  282 us
    reduce_scatter x4, waiting for transfers between devices, micro_batch(): lax.psum_scatter(grad_kv_all, ('col', 'dp'), scatter_dimension=0, tiled=T...  209 us
    while x56, waiting for transfers between devices  175 us
    reduce_scatter x8, waiting for transfers between devices, col_sums(): lax.psum_scatter(lax.dot_general(left, weight, (((1,), (contract,)), ((),...  175 us
    all_gather x8, waiting for transfers between devices, col_rows(): return lax.all_gather(values, 'col', axis=0, tiled=True)  117 us
    psum x16, blocking collectives, row_total(): return lax.psum(values, 'col')  113 us
    all_gather x4, waiting for transfers between devices, micro_batch(): again = lax.all_gather(keys_values, ('col', 'dp'), axis=0, tiled=True)  100 us
    all_gather x8, blocking collectives, col_rows(): return lax.all_gather(values, 'col', axis=0, tiled=True)  75.7 us
  transfers between devices with their start and end apart: 52, of which 47 were waited for; matrix products, arithmetic and copies ran while one was open for 13% of the time, Pallas kernels for 0%

commit v1 on v0

v1 whole, which is shorter than its diff:
```python
import functools

import jax
import jax.numpy as jnp
from jax import lax
from jax.experimental import pallas as pl
from jax.experimental.pallas import tpu as pltpu
from jax.sharding import PartitionSpec as P

HEAD_SIZE = 64
SEG = 256
EPSILON = 1e-05
THETA = 10000.0
MASKED = -1e30
BF = jnp.bfloat16
F32 = jnp.float32


def nt(left, right):
    return lax.dot_general(left, right, (((1,), (1,)), ((), ())), preferred_element_type=F32)


def nn(left, right):
    return lax.dot_general(left, right, (((1,), (0,)), ((), ())), preferred_element_type=F32)


def tn(left, right):
    return lax.dot_general(left, right, (((0,), (0,)), ((), ())), preferred_element_type=F32)


def rope_tables(places):
    halfway = HEAD_SIZE // 2
    inverse = THETA ** (-(jnp.arange(halfway, dtype=F32) * 2.0 / HEAD_SIZE))
    angles = places.astype(F32)[:, None] * inverse[None, :]
    cosine, sine = jnp.cos(angles), jnp.sin(angles)
    return jnp.concatenate([cosine, cosine], -1), jnp.concatenate([sine, sine], -1)


def turned(values):
    halfway = HEAD_SIZE // 2
    return jnp.concatenate([-values[..., halfway:], values[..., :halfway]], axis=-1)


def rotate(values, cosine, sine):
    return values * cosine[:, None, :] + turned(values) * sine[:, None, :]


def unrotate(values, cosine, sine):
    return values * cosine[:, None, :] - turned(values * sine[:, None, :])


def block_mask(starts, bounds, segment, width):
    group = width // SEG
    bound = jnp.concatenate([bounds] * group, axis=1)
    place = starts[segment] + lax.broadcasted_iota(jnp.int32, (SEG, width), 0)
    return place < bound


def attend_kernel(segments, starts, bounds, q_ref, k_ref, v_ref, o_ref, log_ref, s_ref):
    q = q_ref[0]
    width = q.shape[0]
    scale = HEAD_SIZE ** (-0.5)
    highest = jnp.full((1, width), MASKED, F32)

    def score(j, highest):
        rows = pl.ds(pl.multiple_of(j * SEG, SEG), SEG)
        s = nt(k_ref[0, rows], q) * scale
        s = jnp.where(block_mask(starts, bounds[...], j, width), s, MASKED)
        s_ref[rows] = s
        return jnp.maximum(highest, jnp.max(s, axis=0, keepdims=True))

    highest = lax.fori_loop(0, segments, score, highest)

    def total(j, summed):
        rows = pl.ds(pl.multiple_of(j * SEG, SEG), SEG)
        p = jnp.exp(s_ref[rows] - highest)
        s_ref[rows] = p
        return summed + jnp.sum(p, axis=0, keepdims=True)

    summed = lax.fori_loop(0, segments, total, jnp.zeros((1, width), F32))
    inverse = 1.0 / summed

    def weigh(j, out):
        rows = pl.ds(pl.multiple_of(j * SEG, SEG), SEG)
        p = (s_ref[rows] * inverse).astype(BF)
        return out + tn(v_ref[0, rows], p)

    out = lax.fori_loop(0, segments, weigh, jnp.zeros((HEAD_SIZE, width), F32))
    o_ref[0] = out.T.astype(BF)
    log_ref[0] = highest + jnp.log(summed)


def attend_back_kernel(
    segments, starts, bounds, q_ref, k_ref, v_ref, do_ref, log_ref, delta_ref, dq_ref, dk_ref, dv_ref
):
    q, do = q_ref[0], do_ref[0]
    width = q.shape[0]
    scale = HEAD_SIZE ** (-0.5)
    logs, delta = log_ref[0], delta_ref[0]

    def visit(j, grad_q):
        rows = pl.ds(pl.multiple_of(j * SEG, SEG), SEG)
        k = k_ref[0, rows]
        s = nt(k, q) * scale
        s = jnp.where(block_mask(starts, bounds[...], j, width), s, MASKED)
        p = jnp.exp(s - logs)
        dp = nt(v_ref[0, rows], do)
        ds = (p * (dp - delta)).astype(BF)
        dk_ref[0, rows] = nn(ds, q) * scale
        dv_ref[0, rows] = nn(p.astype(BF), do)
        return grad_q + tn(k, ds)

    grad_q = lax.fori_loop(0, segments, visit, jnp.zeros((HEAD_SIZE, width), F32))
    dq_ref[0] = grad_q.T * scale


def head_spec(rows, last=HEAD_SIZE):
    return pl.BlockSpec((1, rows, last), lambda g, *_: (g, 0, 0))


def attend(starts, bounds, q, k, v):
    heads, width, _ = q.shape
    keys = k.shape[1]
    return pl.pallas_call(
        functools.partial(attend_kernel, keys // SEG),
        grid_spec=pltpu.PrefetchScalarGridSpec(
            num_scalar_prefetch=1,
            grid=(heads,),
            in_specs=[
                pl.BlockSpec((1, SEG), lambda g, *_: (0, 0)),
                head_spec(width),
                head_spec(keys),
                head_spec(keys),
            ],
            out_specs=[head_spec(width), head_spec(1, width)],
            scratch_shapes=[pltpu.VMEM((keys, width), F32)],
        ),
        out_shape=[
            jax.ShapeDtypeStruct(q.shape, BF),
            jax.ShapeDtypeStruct((heads, 1, width), F32),
        ],
        compiler_params=pltpu.CompilerParams(vmem_limit_bytes=60 << 20),
        name="attend",
    )(starts, bounds, q, k, v)


def attend_back(starts, bounds, q, k, v, do, logs, delta):
    heads, width, _ = q.shape
    keys = k.shape[1]
    return pl.pallas_call(
        functools.partial(attend_back_kernel, keys // SEG),
        grid_spec=pltpu.PrefetchScalarGridSpec(
            num_scalar_prefetch=1,
            grid=(heads,),
            in_specs=[
                pl.BlockSpec((1, SEG), lambda g, *_: (0, 0)),
                head_spec(width),
                head_spec(keys),
                head_spec(keys),
                head_spec(width),
                head_spec(1, width),
                head_spec(1, width),
            ],
            out_specs=[head_spec(width), head_spec(keys), head_spec(keys)],
        ),
        out_shape=[
            jax.ShapeDtypeStruct(q.shape, F32),
            jax.ShapeDtypeStruct(k.shape, F32),
            jax.ShapeDtypeStruct(k.shape, F32),
        ],
        compiler_params=pltpu.CompilerParams(vmem_limit_bytes=60 << 20),
        name="attend_back",
    )(starts, bounds, q, k, v, do, logs, delta)


def norm_forward(values):
    width = values.shape[1]
    scale = lax.rsqrt(jnp.sum(values * values, axis=1, keepdims=True) / width + EPSILON)
    return values * scale, scale


def norm_backward(normed, scale, gain, grad_normed):
    width = normed.shape[1]
    weighted = grad_normed * gain
    inner = jnp.sum(weighted * normed, axis=1, keepdims=True) / width
    return scale * (weighted - normed * inner), jnp.sum(grad_normed * normed, axis=0)


def shards(
    tokens,
    positions,
    prefix,
    norm1_gain,
    qkv_part,
    out_part,
    norm2_gain,
    gate_up_part,
    down_part,
    cotangent,
):
    rows_count, col_count, data_count = (lax.axis_size(a) for a in ("row", "col", "dp"))
    row, col, data = (lax.axis_index(a) for a in ("row", "col", "dp"))
    both = ("col", "dp")
    part = tokens.shape[1]
    width = part * col_count
    sequences = tokens.shape[0] // SEG
    per_row = sequences // rows_count
    assert per_row == col_count
    sequence = row * col_count + col
    query_heads = out_part.shape[0] // HEAD_SIZE
    kv_heads = (qkv_part.shape[1] // HEAD_SIZE - query_heads) // 2
    group = query_heads // kv_heads
    hidden = down_part.shape[0]

    gain_one = lax.all_gather(norm1_gain, both, axis=0, tiled=True).astype(F32)
    gain_two = lax.all_gather(norm2_gain, both, axis=0, tiled=True).astype(F32)
    qkv = lax.all_gather(qkv_part, ("row",) + both, axis=0, tiled=True)
    qkv = qkv.reshape(rows_count, width, qkv_part.shape[1])
    out_t = lax.all_gather(out_part.T, ("row",) + both, axis=0, tiled=True)
    out_t = out_t.reshape(rows_count, width, out_part.shape[0])
    gate_up = lax.all_gather(gate_up_part, both, axis=0, tiled=True)
    down_t = lax.all_gather(down_part.T, both, axis=0, tiled=True)

    mine = lax.dynamic_slice_in_dim(
        tokens.reshape(sequences, SEG, part), row * per_row, per_row, axis=0
    )
    mine = lax.all_to_all(mine, "col", 0, 0)
    x = mine.transpose(1, 0, 2).reshape(SEG, width).astype(F32)
    cot = lax.all_to_all(cotangent.reshape(rows_count, per_row, SEG, part), "col", 1, 1)
    cot = cot.transpose(0, 2, 1, 3).reshape(rows_count, SEG, width)
    cot_mine = lax.dynamic_index_in_dim(cot, row, 0, keepdims=False)
    cot_pair = cot.reshape(rows_count * SEG, width)

    starts_all = lax.all_gather(positions.reshape(sequences, SEG)[:, 0], "dp", axis=0)
    starts = lax.dynamic_index_in_dim(starts_all, sequence, 1, keepdims=False)
    limit = lax.dynamic_index_in_dim(prefix, sequence, 0, keepdims=False)
    places = lax.dynamic_index_in_dim(starts, data, 0, keepdims=False) + jnp.arange(
        SEG, dtype=jnp.int32
    )
    bounds = jnp.maximum(places + 1, limit)[None, :]
    cosine, sine = rope_tables(places)

    normed_one, scale_one = norm_forward(x)
    input_one = (normed_one * gain_one).astype(BF)
    queries, keys, values = [], [], []
    for r in range(rows_count):
        mixed = nn(input_one, qkv[r]).reshape(SEG, query_heads + 2 * kv_heads, HEAD_SIZE)
        queries.append(rotate(mixed[:, :query_heads], cosine, sine).astype(BF))
        keys.append(
            rotate(mixed[:, query_heads : query_heads + kv_heads], cosine, sine).astype(BF)
        )
        values.append(mixed[:, query_heads + kv_heads :].astype(BF))
    all_kv = rows_count * kv_heads
    q = jnp.concatenate(queries, 1).reshape(SEG, all_kv, group, HEAD_SIZE)
    q = q.transpose(1, 2, 0, 3).reshape(all_kv, group * SEG, HEAD_SIZE)
    kv = jnp.concatenate(keys + values, 1).reshape(SEG, 2 * all_kv * HEAD_SIZE)
    everyone = lax.all_gather(kv, "dp", axis=0, tiled=True)
    everyone = everyone.reshape(data_count * SEG, 2 * all_kv, HEAD_SIZE).transpose(1, 0, 2)
    k, v = everyone[:all_kv], everyone[all_kv:]
    heads, logs = attend(starts, bounds, q, k, v)
    heads_flat = heads.reshape(all_kv, group, SEG, HEAD_SIZE).transpose(2, 0, 1, 3)
    heads_flat = heads_flat.reshape(SEG, rows_count, query_heads * HEAD_SIZE)
    middle = x
    for r in range(rows_count):
        middle = middle + nt(heads_flat[:, r], out_t[r])
    normed_two, scale_two = norm_forward(middle)
    input_two = (normed_two * gain_two).astype(BF)

    pair = lax.all_gather(input_two, "row", axis=0, tiled=True)
    mix = nn(pair, gate_up)
    gate, upward = mix[:, :hidden], mix[:, hidden:]
    sigma = jax.nn.sigmoid(gate)
    active = (gate * sigma * upward).astype(BF)
    result = nt(active, down_t)
    result = middle + lax.psum_scatter(
        result.astype(BF), "row", scatter_dimension=0, tiled=True
    ).astype(F32)
    grad_down = tn(cot_pair, active)
    grad_active = nn(cot_pair, down_t)
    grad_gate = grad_active * upward * sigma * (1.0 + gate * (1.0 - sigma))
    grad_mix = jnp.concatenate([grad_gate, grad_active * gate * sigma], axis=1).astype(BF)
    grad_gate_up = tn(pair, grad_mix)
    grad_normed_two = lax.psum_scatter(
        nt(grad_mix, gate_up).astype(BF), "row", scatter_dimension=0, tiled=True
    ).astype(F32)
    back_two, grad_gain_two = norm_backward(normed_two, scale_two, gain_two, grad_normed_two)
    grad_middle = cot_mine.astype(F32) + back_two
    branch = grad_middle.astype(BF)
    grad_heads, grad_out = [], []
    for r in range(rows_count):
        grad_out.append(tn(branch, heads_flat[:, r]))
        grad_heads.append(nn(branch, out_t[r]).astype(BF))
    do = jnp.concatenate(grad_heads, 1).reshape(SEG, all_kv, group, HEAD_SIZE)
    do = do.transpose(1, 2, 0, 3).reshape(all_kv, group * SEG, HEAD_SIZE)
    delta = jnp.sum(do.astype(F32) * heads.astype(F32), axis=-1)[:, None, :]
    dq, dk, dv = attend_back(starts, bounds, q, k, v, do, logs, delta)
    dkv = jnp.concatenate([dk, dv], 0).transpose(1, 0, 2)
    dkv = dkv.reshape(data_count * SEG, 2 * all_kv * HEAD_SIZE).astype(BF)
    dkv = lax.psum_scatter(dkv, "dp", scatter_dimension=0, tiled=True).astype(F32)
    dkv = dkv.reshape(SEG, 2 * all_kv, HEAD_SIZE)
    dk, dv = unrotate(dkv[:, :all_kv], cosine, sine), dkv[:, all_kv:]
    dq = dq.reshape(all_kv, group, SEG, HEAD_SIZE).transpose(2, 0, 1, 3)
    dq = unrotate(dq.reshape(SEG, all_kv * group, HEAD_SIZE), cosine, sine)
    grad_qkv, grad_normed_one = [], 0.0
    for r in range(rows_count):
        ours = slice(r * kv_heads, (r + 1) * kv_heads)
        grad_mixed = jnp.concatenate(
            [dq[:, r * query_heads : (r + 1) * query_heads], dk[:, ours], dv[:, ours]], 1
        )
        grad_mixed = grad_mixed.reshape(SEG, qkv_part.shape[1]).astype(BF)
        grad_qkv.append(tn(input_one, grad_mixed))
        grad_normed_one = grad_normed_one + nt(grad_mixed, qkv[r])
    back_one, grad_gain_one = norm_backward(normed_one, scale_one, gain_one, grad_normed_one)
    grad_input = grad_middle + back_one

    def to_output(values):
        pieces = values.astype(BF).reshape(SEG, col_count, part).transpose(1, 0, 2)
        pieces = lax.all_to_all(pieces, "col", 0, 0)
        return lax.all_gather(pieces, "row", axis=0, tiled=True).reshape(sequences * SEG, part)

    def sum_half(parts):
        halves = lax.psum_scatter(
            jnp.stack(parts).astype(BF), "row", scatter_dimension=0, tiled=True
        )
        halves = halves.reshape(halves.shape[1:])
        return lax.psum_scatter(halves, both, scatter_dimension=0, tiled=True).astype(F32)

    def sum_whole(values):
        return lax.psum_scatter(values.astype(BF), both, scatter_dimension=0, tiled=True).astype(
            F32
        )

    gains = lax.psum(jnp.stack([grad_gain_one, grad_gain_two]), ("row",) + both)
    gains = lax.dynamic_slice_in_dim(
        gains, (col * data_count + data) * norm1_gain.shape[0], norm1_gain.shape[0], axis=1
    )
    return (
        to_output(result),
        to_output(grad_input).astype(F32),
        gains[0],
        sum_half(grad_qkv),
        sum_half(grad_out).T,
        gains[1],
        sum_whole(grad_gate_up),
        sum_whole(grad_down).T,
    )


def solution(mesh):
    both = ("col", "dp")
    in_specs = (
        P("dp", "col"),
        P("dp"),
        P(),
        P(both),
        P(both, "row"),
        P("row", both),
        P(both),
        P(both, "row"),
        P("row", both),
        P("dp", "col"),
    )
    out_specs = (
        P("dp", "col"),
        P("dp", "col"),
        P(both),
        P(both, "row"),
        P("row", both),
        P(both),
        P(both, "row"),
        P("row", both),
    )
    return jax.shard_map(shards, mesh=mesh, in_specs=in_specs, out_specs=out_specs, check_vma=False)
```

time: 2250 us -> 968 us (0.43)
  waiting for transfers between devices: 1180 us -> 596 us
  blocking collectives: 416 us -> 121 us
  other arithmetic: 186 us -> 33.3 us
  matrix products: 210 us -> 62.6 us
  local copies, waits for them, and re-layouts: 177 us -> 79.4 us
  loops' own time: 52.7 us -> 0 us
  Pallas kernels: 0 us -> 39.8 us
    psum x12 -> x0, waiting for transfers between devices: 282 us -> none  [row_sum(): return lax.psum(values.astype(jnp.bfloat16), 'row').astype(jnp.float32)]
    reduce_scatter x15 -> x6, waiting for transfers between devices: 467 us -> 187 us  [the longest x1 92.6 us: sum_whole(): lax.psum_scatter(values.astype(BF), both, scatter_dimension=0, tiled=True)]
    all_gather x21 -> x0, blocking collectives: 260 us -> none  [the longest x8 75.7 us: col_rows(): return lax.all_gather(values, 'col', axis=0, tiled=True)]
    unnamed x5 -> x20, waiting for transfers between devices: 0.07 us -> 223 us
    while x56 -> x0, waiting for transfers between devices: 175 us -> none
    dot_general x160 -> x18, matrix products: 210 us -> 62.6 us  [the longest x6 25.8 us: nn(): lax.dot_general(left, right, (((1,), (0,)), ((), ())), preferred_element_...]
    all_gather x16 -> x8, waiting for transfers between devices: 257 us -> 185 us  [the longest x1 65.1 us: shards(): gate_up = lax.all_gather(gate_up_part, both, axis=0, tiled=True)]
    psum x16 -> x1, blocking collectives: 113 us -> 41.9 us  [shards(): gains = lax.psum(jnp.stack([grad_gain_one, grad_gain_two]), ('row',) + both)]
  transfers between devices with their start and end apart: 52 -> 18, of which waited for: 47 -> 14; matrix products, arithmetic and copies ran while one was open for 13% -> 11% of each run, Pallas kernels for 0% -> 2%
where the time goes in v1:
time: 968 us; the launch traced here: 954 us
  waiting for transfers between devices  596 us (62%)
  blocking collectives  121 us (12%)
  local copies, waits for them, and re-layouts  79.4 us (8%)
  matrix products  62.6 us (6%)
  Pallas kernels  39.8 us (4%)
  other arithmetic  33.3 us (3%)
  between operations  17.2 us (2%)
    unnamed x20, waiting for transfers between devices  223 us
    reduce_scatter x1, waiting for transfers between devices, sum_whole(): lax.psum_scatter(values.astype(BF), both, scatter_dimension=0, tiled=True)  92.6 us
    all_gather x1, waiting for transfers between devices, shards(): gate_up = lax.all_gather(gate_up_part, both, axis=0, tiled=True)  65.1 us
    reduce_scatter x2, waiting for transfers between devices, sum_half(): lax.psum_scatter(jnp.stack(parts).astype(BF), 'row', scatter_dimension=0,...  57.8 us
    psum x1, blocking collectives, shards(): gains = lax.psum(jnp.stack([grad_gain_one, grad_gain_two]), ('row',) + both)  41.9 us
    all_gather x1, waiting for transfers between devices, shards(): down_t = lax.all_gather(down_part.T, both, axis=0, tiled=True)  37.9 us
    all_gather x1, waiting for transfers between devices, shards(): out_t = lax.all_gather(out_part.T, ('row',) + both, axis=0, tiled=True)  36.8 us
    unnamed x2, blocking collectives  36.6 us
  transfers between devices with their start and end apart: 18, of which 14 were waited for; matrix products, arithmetic and copies ran while one was open for 11% of the time, Pallas kernels for 2%

profile of v1, /device:TPU:13, one launch (start us, length us, event | category | flops | bytes accessed | tf_op | source)
XLA Modules:
  0.0 954.3 jit_solution(6545804611306380562)
XLA Ops:
  17.4 28.4 %all-reduce.4 = (bf16[1152]{0:T(1024)(128)(2,1)S(1)}, bf16[1152]{0:T(1024)(128)(2,1)S(1)}) all-reduce(bf16[1152]{0:T(1024)(128)(2,1)S(1)} %dynamic-update-slice.1, bf16[1152]{0:T(1024)(128)(2,1)S(1)} %dynamic-update-slice.2), channel_id=1, replica_groups=mesh['row'=2,'col'=4,'dp'=4] {'col','dp'}, use_global_device_ids=true, to_apply=%add.1 | all-reduce | flops 2304 | bytes 9216
  47.5 8.2 all-reduce
  58.7 17.6 %all-gather.10.cloned.1.call-done = bf16[2304,960]{1,0:T(8,128)(2,1)} async-done(((bf16[72,960]{1,0:T(8,128)(2,1)}), bf16[2304,960]{1,0:T(8,128)(2,1)}) %all-gather.10.cloned.1.call-update) | async-done | bytes 4423696 | tf_op jit(solution)/shard_map/all_gather | solution.py:217
  76.2 4.3 slice_bitcast_fusion.1
  80.5 4.3 copy.102
  104.3 24.3 %all-gather.12.cloned.1.call-done = bf16[1024,768]{0,1:T(8,128)(2,1)} async-done(((bf16[256,768]{0,1:T(8,128)(2,1)}), bf16[1024,768]{0,1:T(8,128)(2,1)}) %all-gather.12.cloned.1.call-update) | async-done | bytes 1572880 | tf_op jit(solution)/shard_map/all_gather | solution.py:257
  133.5 18.6 %attend.1 = (bf16[6,768,64]{2,1,0:T(8,128)(2,1)}, f32[6,1,768]{2,1,0:T(1,128)}) custom-call(s32[4]{0:T(128)} %dynamic-slice_reduce_fusion.starts, s32[1,256]{1,0:T(1,128)} %add_maximum_fusion.bounds, bf16[6,768,64]{2,1,0:T(8,128)(2,1)} %bitcast.145, bf16[6,1024,64]{2,1,0:T(8,128)(2,1)} %get-tuple-element.70.k_ref, bf16[6,1024,64]{2,1,0:T(8,128)(2,1)} %get-tuple-element.69.v_ref), custom_call_target="tpu_custom_call" | custom-call | tf_op jit(solution)/shard_map/attend/pallas_call | solution.py:124
  153.8 36.8 %all-gather.14.cloned.1.call-done = bf16[2304,576]{1,0:T(8,128)(2,1)} async-done(((bf16[72,576]{1,0:T(8,128)(2,1)}), bf16[2304,576]{1,0:T(8,128)(2,1)}) %all-gather.14.cloned.1.call-update) | async-done | bytes 2654224 | tf_op jit(solution)/shard_map/all_gather | solution.py:219
  200.4 17.2 %all_to_all.20 = bf16[2,4,256,288]{2,0,3,1:T(2,128)(2,1)S(1)} all-to-all(bf16[2,4,256,288]{2,0,3,1:T(2,128)(2,1)S(1)} %copy.112), channel_id=1, replica_groups=mesh['row'=2,'col'=4,'dp'=4] {'col'}, dimensions={1} | all-to-all | bytes 2359296 | tf_op jit(solution)/shard_map/all_to_all | solution.py:229
  220.4 65.1 %all-gather.18.cloned.1.call-done = bf16[1152,3072]{1,0:T(8,128)(2,1)} async-done(((bf16[72,3072]{1,0:T(8,128)(2,1)}), bf16[1152,3072]{1,0:T(8,128)(2,1)}) %all-gather.18.cloned.1.call-update) | async-done | bytes 7077904 | tf_op jit(solution)/shard_map/all_gather | solution.py:221
  285.5 10.3 %fusion.45 = f32[512,3072]{1,0:T(8,128)} fusion(bf16[512,1152]{1,0:T(8,128)(2,1)} %all-gather.16.cloned.1.call-done, bf16[1152,3072]{1,0:T(8,128)(2,1)} %all-gather.18.cloned.1.call-done), kind=kOutput, calls=%fused_computation.124 | convolution fusion | flops 3623878656 | bytes 14548992 | tf_op jit(solution)/shard_map/dot_general | solution.py:24
  295.8 37.9 %all-gather.20.cloned.1.call-done = bf16[1152,1536]{1,0:T(8,128)(2,1)} async-done(((bf16[72,1536]{1,0:T(8,128)(2,1)}), bf16[1152,1536]{1,0:T(8,128)(2,1)}) %all-gather.20.cloned.1.call-update) | async-done | bytes 3538960 | tf_op jit(solution)/shard_map/all_gather | solution.py:222
  333.7 9.1 multiply_convert_fusion.1
  344.5 5.3 convolution_convert_fusion.7
  352.3 18.3 %reduce-scatter.16.cloned.1.call-done = bf16[256,1152]{1,0:T(8,128)(2,1)} async-done(((bf16[512,1152]{1,0:T(8,128)(2,1)}), bf16[256,1152]{1,0:T(8,128)(2,1)}) %reduce-scatter.16.cloned.1.call-update) | async-done | bytes 589840 | tf_op jit(solution)/shard_map/reduce_scatter | solution.py:283
  381.0 21.1 %attend_back.1 = (f32[6,768,64]{2,1,0:T(8,128)}, f32[6,1024,64]{2,1,0:T(8,128)}, f32[6,1024,64]{2,1,0:T(8,128)}) custom-call(s32[4]{0:T(128)} %dynamic-slice_reduce_fusion.starts, s32[1,256]{1,0:T(1,128)} %add_maximum_fusion.bounds, bf16[6,768,64]{2,1,0:T(8,128)(2,1)} %bitcast.146, bf16[6,1024,64]{2,1,0:T(8,128)(2,1)} %get-tuple-element.70.k_ref, ...), custom_call_target="tpu_custom_call" | custom-call | tf_op jit(solution)/shard_map/attend_back/pallas_call | solution.py:150
  407.4 4.3 copy.118
  411.8 5.8 convolution_convert_fusion.6
  426.6 18.7 %reduce-scatter.18.cloned.1.call-done = bf16[256,768]{0,1:T(8,128)(2,1)} async-done(((bf16[1024,768]{0,1:T(8,128)(2,1)}), bf16[256,768]{0,1:T(8,128)(2,1)}) %reduce-scatter.18.cloned.1.call-update) | async-done | bytes 393232 | tf_op jit(solution)/shard_map/reduce_scatter | solution.py:299
  454.2 5.7 fusion
  459.8 5.8 copy.133
  469.4 4.5 multiply_reduce_fusion.1
  478.9 12.3 %all_to_all.21 = bf16[4,256,288]{1,2,0:T(8,128)(2,1)} all-to-all(bf16[4,256,288]{1,2,0:T(8,128)(2,1)S(1)} %bitcast.167), channel_id=1, replica_groups=mesh['row'=2,'col'=4,'dp'=4] {'col'}, dimensions={0} | all-to-all | bytes 1179648 | tf_op jit(solution)/shard_map/all_to_all | solution.py:318
  491.6 12.9 %all_to_all.22 = bf16[4,256,288]{1,2,0:T(8,128)(2,1)} all-to-all(bf16[4,256,288]{1,2,0:T(8,128)(2,1)S(1)} %bitcast.168), channel_id=1, replica_groups=mesh['row'=2,'col'=4,'dp'=4] {'col'}, dimensions={0} | all-to-all | bytes 1179648 | tf_op jit(solution)/shard_map/all_to_all | solution.py:318
  504.6 5.8 reduce-scatter.22.cloned.1.call-done
  510.5 7.1 convolution_convert_fusion
  517.7 52.0 %reduce-scatter.20.cloned.1.call-done = bf16[1,1152,960]{1,2,0:T(8,128)(2,1)} async-done(((bf16[2,1152,960]{1,2,0:T(8,128)(2,1)}), bf16[1,1152,960]{1,2,0:T(8,128)(2,1)}) %reduce-scatter.20.cloned.1.call-update) | async-done | bytes 2211856 | tf_op jit(solution)/shard_map/reduce_scatter | solution.py:322
  574.6 64.6 %reduce-scatter.28.cloned.1.call-done = bf16[72,1536]{1,0:T(8,128)(2,1)} async-done(((bf16[1152,1536]{1,0:T(8,128)(2,1)}), bf16[72,1536]{1,0:T(8,128)(2,1)}) %reduce-scatter.28.cloned.1.call-update) | async-done | bytes 221200
  641.4 41.9 %psum.7 = f32[2,1152]{1,0:T(2,128)S(1)} all-reduce(f32[2,1152]{1,0:T(2,128)S(1)} %pad_maximum_fusion.10), channel_id=1, replica_groups=mesh['row'=2,'col'=4,'dp'=4] {'row','col','dp'}, use_global_device_ids=true, to_apply=%region_10.11 | all-reduce | flops 2304 | bytes 18432 | tf_op jit(solution)/shard_map/psum | solution.py:333
  693.1 92.8 %all-reduce.7.cloned.1.call-done = bf16[1152,576]{0,1:T(8,128)(2,1)} async-done(((bf16[1152,576]{0,1:T(8,128)(2,1)}), bf16[1152,576]{0,1:T(8,128)(2,1)}) %all-reduce.7.cloned.1.call-update) | async-done | bytes 1327120
  787.8 92.6 %reduce-scatter.24.cloned.1.call-done = bf16[72,3072]{1,0:T(8,128)(2,1)} async-done(((bf16[1152,3072]{1,0:T(8,128)(2,1)}), bf16[72,3072]{1,0:T(8,128)(2,1)}) %reduce-scatter.24.cloned.1.call-update) | async-done | bytes 442384 | tf_op jit(solution)/shard_map/reduce_scatter | solution.py:329
  882.4 62.9 %reduce-scatter.26.cloned.1.call-done = bf16[72,960]{1,0:T(8,128)(2,1)} async-done(((bf16[1152,960]{1,0:T(8,128)(2,1)}), bf16[72,960]{1,0:T(8,128)(2,1)}) %reduce-scatter.26.cloned.1.call-update) | async-done | bytes 138256
  (255 shorter events, 120.4 us)
Async XLA Ops:
  7.2 69.1 %all-gather.10.cloned.1.call-start = ((), (), s32[]{:S(2)}) async-start(), calls=%async_computation.12 | async-start | bytes 4866048 | tf_op jit(solution)/shard_map/all_gather | solution.py:217
  9.5 6.1 copy-start.43
  9.6 7.3 copy-start.46
  9.6 7.6 copy-start.47
  9.6 36.9 %copy-start.41 = (s32[2048]{0:T(1024)S(1)}, s32[2048]{0:T(1024)}, u32[]{:S(2)}) copy-start(s32[2048]{0:T(1024)} %param.11) | copy-start | bytes 24580
  10.8 47.1 %all-to-all-start = ((bf16[4,256,288]{1,2,0:T(8,128)(2,1)}), bf16[4,256,288]{1,2,0:T(8,128)(2,1)S(1)}, u32[]{:S(2)}, u32[]{:S(2)}) async-start(bf16[4,256,288]{1,2,0:T(8,128)(2,1)} %copy.101), calls=%async_computation | async-start | bytes 1179648 | tf_op jit(solution)/shard_map/all_to_all | solution.py:227
  15.0 113.5 %all-gather.12.cloned.1.call-start = ((), (), s32[]{:S(2)}) async-start(), calls=%async_computation.13 | async-start | bytes 1966080 | tf_op jit(solution)/shard_map/all_gather | solution.py:257
  58.7 32.6 %copy-start.4 = (bf16[4,256,288]{1,2,0:T(8,128)(2,1)}, bf16[4,256,288]{1,2,0:T(8,128)(2,1)S(1)}, u32[]{:S(2)}) copy-start(bf16[4,256,288]{1,2,0:T(8,128)(2,1)S(1)} %multiply_convert_fusion.4) | copy-start | bytes 1769476
  95.7 95.0 %all-gather.14.cloned.1.call-start = ((), (), s32[]{:S(2)}) async-start(), calls=%async_computation.14 | async-start | bytes 3041280 | tf_op jit(solution)/shard_map/all_gather | solution.py:219
  96.4 124.0 %all-gather.16.cloned.1.call-start = ((), (), s32[]{:S(2)}) async-start(), calls=%async_computation.15 | async-start | bytes 1769472 | tf_op jit(solution)/shard_map/all_gather | solution.py:269
  152.1 38.5 %copy-start.1 = (f32[256,1152]{1,0:T(8,128)S(1)}, f32[256,1152]{1,0:T(8,128)}, u32[]{:S(2)}) copy-start(f32[256,1152]{1,0:T(8,128)} %copy.109) | copy-start | bytes 3538948
  153.8 39.1 %copy-start.2 = (bf16[6,3,256,64]{2,3,1,0:T(8,128)(2,1)}, bf16[6,3,256,64]{2,3,1,0:T(8,128)(2,1)S(1)}, u32[]{:S(2)}) copy-start(bf16[6,3,256,64]{2,3,1,0:T(8,128)(2,1)S(1)} %copy.108) | copy-start | bytes 1769476
  195.3 90.2 %all-gather.18.cloned.1.call-start = ((), (), s32[]{:S(2)}) async-start(), calls=%async_computation.16 | async-start | bytes 7520256 | tf_op jit(solution)/shard_map/all_gather | solution.py:221
  195.9 137.8 %all-gather.20.cloned.1.call-start = ((), (), s32[]{:S(2)}) async-start(), calls=%async_computation.17 | async-start | bytes 3760128 | tf_op jit(solution)/shard_map/all_gather | solution.py:222
  196.5 174.1 %reduce-scatter.16.cloned.1.call-start = ((), (), s32[]{:S(2)}) async-start(), calls=%async_computation.20 | async-start | bytes 1769472 | tf_op jit(solution)/shard_map/reduce_scatter | solution.py:283
  333.7 10.8 %copy-start.44 = (bf16[1152,3072]{1,0:T(8,128)(2,1)S(1)}, bf16[1152,3072]{1,0:T(8,128)(2,1)}, u32[]{:S(2)}) copy-start(bf16[1152,3072]{1,0:T(8,128)(2,1)} %all-gather.18.cloned.1.call-done) | copy-start | bytes 21233668
  349.8 95.5 %reduce-scatter.18.cloned.1.call-start = ((), (), s32[]{:S(2)}) async-start(), calls=%async_computation.21 | async-start | bytes 1966080 | tf_op jit(solution)/shard_map/reduce_scatter | solution.py:299
  352.3 21.1 %copy-start.6 = (bf16[1,256,1152]{2,1,0:T(8,128)(2,1)}, bf16[1,256,1152]{2,1,0:T(8,128)(2,1)S(1)}, u32[]{:S(2)}) copy-start(bf16[1,256,1152]{2,1,0:T(8,128)(2,1)S(1)} %copy.135) | copy-start | bytes 1769476
  411.7 62.8 %reduce-scatter.14.cloned.1.call-start = ((), (), s32[]{:S(2)}) async-start(), calls=%async_computation.18 | async-start | bytes 1769472 | tf_op jit(solution)/shard_map/reduce_scatter | solution.py:275
  417.6 92.9 %reduce-scatter.22.cloned.1.call-start = ((), (), s32[]{:S(2)}) async-start(), calls=%async_computation.24 | async-start | bytes 3981312 | tf_op jit(solution)/shard_map/reduce_scatter | solution.py:322
  421.6 148.1 %reduce-scatter.20.cloned.1.call-start = ((), (), s32[]{:S(2)}) async-start(), calls=%async_computation.23 | async-start | bytes 6635520 | tf_op jit(solution)/shard_map/reduce_scatter | solution.py:322
  425.8 21.7 %copy-start.28 = (f32[256,64]{0,1:T(8,128)S(1)}, f32[256,64]{0,1:T(8,128)}, u32[]{:S(2)}) copy-start(f32[256,64]{0,1:T(8,128)} %get-tuple-element.107) | copy-start | bytes 196612
  452.9 186.2 %reduce-scatter.28.cloned.1.call-start = ((), (), s32[]{:S(2)}) async-start(), calls=%async_computation.27 | async-start | bytes 3760128
  465.7 218.2 %all-gather.22.cloned.1.call-start = ((), (), s32[]{:S(2)}) async-start(), calls=%async_computation.19 | async-start | bytes 1769472 | tf_op jit(solution)/shard_map/all_gather | solution.py:319
  477.6 13.8 %copy-start.19 = (bf16[256,1152]{1,0:T(8,128)(2,1)S(1)}, bf16[256,1152]{1,0:T(8,128)(2,1)}, u32[]{:S(2)}) copy-start(bf16[256,1152]{1,0:T(8,128)(2,1)} %get-tuple-element.71) | copy-start | bytes 1769476
  491.3 198.6 %all-gather.24.cloned.1.call-start = ((), (), s32[]{:S(2)}) async-start(), calls=%async_computation.22 | async-start | bytes 1769472 | tf_op jit(solution)/shard_map/all_gather | solution.py:319
  491.6 18.9 %copy-start.45 = (bf16[512,1152]{1,0:T(8,128)(2,1)S(1)}, bf16[512,1152]{1,0:T(8,128)(2,1)}, u32[]{:S(2)}) copy-start(bf16[512,1152]{1,0:T(8,128)(2,1)} %all-gather.16.cloned.1.call-done) | copy-start | bytes 3538948
  491.6 18.9 %copy-start.51 = (bf16[512,1536]{1,0:T(8,128)(2,1)S(1)}, bf16[512,1536]{1,0:T(8,128)(2,1)}, u32[]{:S(2)}) copy-start(bf16[512,1536]{1,0:T(8,128)(2,1)} %copy-done.50) | copy-start | bytes 4718596
  504.5 281.4 %all-reduce.7.cloned.1.call-start = ((), (), s32[]{:S(2)}) async-start(), calls=%async_computation.28 | async-start | bytes 2654208
  510.4 370.0 %reduce-scatter.24.cloned.1.call-start = ((), (), s32[]{:S(2)}) async-start(), calls=%async_computation.25 | async-start | bytes 7520256 | tf_op jit(solution)/shard_map/reduce_scatter | solution.py:329
  517.6 427.7 %reduce-scatter.26.cloned.1.call-start = ((), (), s32[]{:S(2)}) async-start(), calls=%async_computation.26 | async-start | bytes 2506752
  573.9 67.5 %copy-start.42 = (f32[1152]{0:T(1024)S(1)}, f32[1152]{0:T(1024)}, u32[]{:S(2)}) copy-start(f32[1152]{0:T(1024)} %get-tuple-element.58) | copy-start | bytes 13828
  (39 other events, 81.1 us)
Sparse Core Ops, SparseCore 0:
  10.9 65.3 all-gather.9
  95.8 32.7 all-gather.11
  131.4 59.1 all-gather.13
  195.4 22.0 all-gather.15
  219.7 65.7 all-gather.17
  287.6 46.0 all-gather.19
  349.9 20.5 reduce-scatter.15
  411.8 33.4 reduce-scatter.17
  447.6 22.6 reduce-scatter.13
  472.4 38.0 reduce-scatter.21
  512.7 56.8 reduce-scatter.19
  573.4 65.7 reduce-scatter.27
  640.7 24.1 all-gather.21
  666.3 23.5 all-gather.23
  693.2 92.6 all-reduce.6
  789.8 90.6 reduce-scatter.23
  884.0 61.2 reduce-scatter.25
